TPU v7x, 256 devices: a whole 4x4x8 slice. The times are simulated.
256 devices in a mesh: row: 16 (over x_lo, z), col: 16 (over x_hi, y, core).
Axes of the slice: x: 4 (x_hi: 2, x_lo: 2; x = x_hi * 2 + x_lo), y: 4, z: 8, core: 2. Of those that a mesh axis runs over, the one named last changes fastest.
Arguments:
- tensor: bfloat16 [4096, 2048, 128], P('row', 'col'), may hold values from -96 to 96
- factor_a: float32 [4096, 128], P(('row', 'col')), may hold values from -4.5 to 4.5
- factor_b: float32 [2048, 128], P(('col', 'row')), may hold values from -4.5 to 4.5
- factor_c: float32 [128, 128], replicated, may hold values from -4.5 to 4.5
Outputs:
- new_a: float32 [4096, 128], P(('row', 'col'))
- new_b: float32 [2048, 128], P(('col', 'row'))
- new_c: float32 [128, 128], replicated
All inputs are finite; a program needn't handle non-finite values.
Results may differ from a plain program's by a relative error of at most 0.01.
Values may be sent and summed in bfloat16 or wider, within the bound.
A program may use at most 128 MiB of HBM per device.

v0:
```python
import jax
import jax.numpy as jnp
from jax import lax
from jax.sharding import PartitionSpec as P

STEPS = 2


damping = 0.9
scaling = 0.25
epsilon = 1e-06


def column_squares(values16):
    return jnp.sum(jnp.square(values16.astype(jnp.float32)), axis=0)


def local_terms(block, tile_a, tile_b, c16):
    rows_i, rows_j, depth = block.shape
    rank = tile_a.shape[1]
    pairs = (
        tile_a.astype(jnp.float32)[:, None, :] * tile_b.astype(jnp.float32)[None, :, :]
    ).astype(jnp.bfloat16)
    pairs = pairs.reshape(rows_i * rows_j, rank)
    model = jnp.dot(pairs, c16.T, preferred_element_type=jnp.float32)
    resid = (block.reshape(rows_i * rows_j, depth).astype(jnp.float32) - model).astype(jnp.bfloat16)
    along = jnp.dot(resid, c16, preferred_element_type=jnp.float32).reshape(rows_i, rows_j, rank)
    grad_a = jnp.sum(along * tile_b.astype(jnp.float32)[None, :, :], axis=1)
    grad_b = jnp.sum(along * tile_a.astype(jnp.float32)[:, None, :], axis=0)
    grad_c = lax.dot_general(
        resid, pairs, (((0,), (0,)), ((), ())), preferred_element_type=jnp.float32
    )
    return (grad_a, grad_b, grad_c)


def local(tensor, factor_a, factor_b, factor_c):
    own_a, own_b, third = (factor_a, factor_b, factor_c)
    for step in range(STEPS):
        a_mine16 = own_a.astype(jnp.bfloat16)
        b_mine16 = own_b.astype(jnp.bfloat16)
        tile_a = lax.all_gather(a_mine16, "col", axis=0, tiled=True)
        tile_b = lax.all_gather(b_mine16, "row", axis=0, tiled=True)
        norm_a, norm_b = lax.psum(
            (column_squares(a_mine16), column_squares(b_mine16)), ("row", "col")
        )
        c16 = third.astype(jnp.bfloat16)
        norm_c = column_squares(c16)
        step_a = scaling / (norm_b * norm_c + epsilon)
        step_b = scaling / (norm_a * norm_c + epsilon)
        step_c = scaling / (norm_a * norm_b + epsilon)
        grad_a, grad_b, grad_c = local_terms(tensor, tile_a, tile_b, c16)
        grad_a = lax.psum_scatter(
            grad_a.astype(jnp.bfloat16), "col", scatter_dimension=0, tiled=True
        ).astype(jnp.float32)
        grad_b = lax.psum_scatter(
            grad_b.astype(jnp.bfloat16), "row", scatter_dimension=0, tiled=True
        ).astype(jnp.float32)
        own_a = damping * own_a + step_a * grad_a
        own_b = damping * own_b + step_b * grad_b
        grad_c = lax.psum(grad_c, ("row", "col"))
        third = damping * third + step_c * grad_c
    return (own_a, own_b, third)


def solution(mesh):
    return jax.shard_map(
        local,
        mesh=mesh,
        in_specs=(P("row", "col", None), P(("row", "col"), None), P(("col", "row"), None), P()),
        out_specs=(P(("row", "col"), None), P(("col", "row"), None), P()),
        check_vma=False,
    )
```

profile of v0, /device:TPU:1, one launch (start us, length us, event | category | flops | bytes accessed | tf_op | source)
XLA Modules:
  0.0 663.4 jit_solution(11993279583761159699)
XLA Ops:
  8.1 0.7 multiply_reduce_fusion.9
  8.8 0.7 multiply_reduce_fusion.7
  9.5 30.3 %all_gather.13 = bf16[128,128]{1,0:T(8,128)(2,1)S(1)} all-gather(bf16[8,128]{1,0:T(8,128)(2,1)S(1)} %get-tuple-element.14), channel_id=1, replica_groups=mesh['row'=16,'col'=16] {'row'}, dimensions={0}, use_global_device_ids=true | all-gather | bytes 34816 | tf_op jit(solution)/shard_map/all_gather | solution.py:42
  39.8 31.7 %all_gather.12 = bf16[256,128]{1,0:T(8,128)(2,1)S(1)} all-gather(bf16[16,128]{1,0:T(8,128)(2,1)S(1)} %get-tuple-element.16), channel_id=1, replica_groups=mesh['row'=16,'col'=16] {'col'}, dimensions={0}, use_global_device_ids=true | all-gather | bytes 69632 | tf_op jit(solution)/shard_map/all_gather | solution.py:41
  71.5 5.6 multiply_convert_fusion.1
  77.1 8.1 %fusion.1 = bf16[32768,128]{1,0:T(8,128)(2,1)S(1)} fusion(bf16[32768,128]{1,0:T(8,128)(2,1)} %bitcast.21, bf16[32768,128]{1,0:T(8,128)(2,1)} %bitcast.25, f32[128,128]{1,0:T(8,128)S(1)} %copy-done.2), kind=kOutput, calls=%fused_computation.3 | convolution fusion | flops 1086341120 | bytes 25231360 | tf_op jit(solution)/shard_map/dot_general | solution.py:25
  85.2 3.2 copy-done
  88.5 6.4 fusion.11
  94.9 0.0 reduce-scatter.3.cloned.1.call-start
  94.9 12.1 %multiply_reduce_fusion.3 = (bf16[256,128]{1,0:T(8,128)(2,1)}, f32[32768,128]{1,0:T(8,128)}) fusion(f32[128,128]{1,0:T(8,128)S(1)} %convert_element_type.111, bf16[32768,128]{1,0:T(8,128)(2,1)} %copy-done, f32[128,128]{1,0:T(8,128)S(1)} %copy-done.2), kind=kOutput, calls=%fused_computation.8 | convolution fusion | flops 1082114048 | bytes 25362432 | tf_op jit(solution)/shard_map/dot_general | solution.py:27
  107.1 7.3 %multiply_reduce_fusion.2 = bf16[128,128]{1,0:T(8,128)(2,1)S(1)} fusion(f32[256,128,128]{2,1,0:T(8,128)} %bitcast.23, f32[256,128]{1,0:T(8,128)S(1)} %convert_element_type.110), kind=kLoop, calls=%fused_computation.7 | loop fusion | flops 8372224 | bytes 16941056 | tf_op jit(solution)/shard_map/reduce_sum | solution.py:29
  114.5 46.3 %all-reduce = bf16[128,128]{1,0:T(8,128)(2,1)S(1)} all-reduce(bf16[128,128]{1,0:T(8,128)(2,1)S(1)} %multiply_reduce_fusion.2), channel_id=3, replica_groups=mesh['row'=16,'col'=16] {'row'}, use_global_device_ids=true, to_apply=%region_8.0.clone | all-reduce | flops 16384 | bytes 65536
  160.8 0.6 dynamic-slice
  162.0 84.4 %all-reduce.3 = (f32[128]{0:T(128)S(1)}, f32[128]{0:T(128)S(1)}) all-reduce(f32[128]{0:T(128)S(1)} %get-tuple-element.15, f32[128]{0:T(128)S(1)} %get-tuple-element.13), channel_id=1, replica_groups=mesh['row'=16,'col'=16] {'row','col'}, use_global_device_ids=true, to_apply=%region_6.0 | all-reduce | flops 256 | bytes 2048 | tf_op jit(solution)/shard_map/psum | solution.py:43
  246.4 81.7 %all-reduce.7.cloned.1.call-done = f32[128,128]{1,0:T(8,128)} async-done(((f32[128,128]{1,0:T(8,128)}), f32[128,128]{1,0:T(8,128)}) %all-reduce.7.cloned.1.call-update) | async-done | bytes 65552 | tf_op jit(solution)/shard_map/psum | solution.py:60
  328.1 0.9 multiply_reduce_fusion.4
  329.1 24.4 %all_gather.15 = bf16[128,128]{1,0:T(8,128)(2,1)S(1)} all-gather(bf16[8,128]{1,0:T(8,128)(2,1)S(1)} %get-tuple-element.12), channel_id=1, replica_groups=mesh['row'=16,'col'=16] {'row'}, dimensions={0}, use_global_device_ids=true | all-gather | bytes 34816 | tf_op jit(solution)/shard_map/all_gather | solution.py:42
  353.5 0.7 multiply_reduce_fusion.6
  354.2 28.8 %all_gather.14 = bf16[256,128]{1,0:T(8,128)(2,1)S(1)} all-gather(bf16[16,128]{1,0:T(8,128)(2,1)S(1)} %get-tuple-element.10), channel_id=1, replica_groups=mesh['row'=16,'col'=16] {'col'}, dimensions={0}, use_global_device_ids=true | all-gather | bytes 69632 | tf_op jit(solution)/shard_map/all_gather | solution.py:41
  383.0 5.6 multiply_convert_fusion
  388.6 8.1 %fusion = bf16[32768,128]{1,0:T(8,128)(2,1)S(1)} fusion(bf16[32768,128]{1,0:T(8,128)(2,1)} %bitcast.19, bf16[128,128]{1,0:T(8,128)(2,1)S(1)} %get-tuple-element.8, bf16[32768,128]{1,0:T(8,128)(2,1)} %bitcast.26), kind=kOutput, calls=%fused_computation.1 | convolution fusion | flops 1086324736 | bytes 25198592 | tf_op jit(solution)/shard_map/dot_general | solution.py:25
  396.8 3.2 copy-done.1
  400.0 6.4 fusion.12
  406.4 12.1 %multiply_reduce_fusion.1 = (bf16[256,128]{1,0:T(8,128)(2,1)}, f32[32768,128]{1,0:T(8,128)}) fusion(f32[128,128]{1,0:T(8,128)S(1)} %convert_element_type.126, bf16[32768,128]{1,0:T(8,128)(2,1)} %copy-done.1, bf16[128,128]{1,0:T(8,128)(2,1)S(1)} %get-tuple-element.8), kind=kOutput, calls=%fused_computation.5 | convolution fusion | flops 1082097664 | bytes 25329664 | tf_op jit(solution)/shard_map/dot_general | solution.py:27
  418.4 0.0 reduce-scatter.5.cloned.1.call-start
  418.5 7.3 %multiply_reduce_fusion = bf16[128,128]{1,0:T(8,128)(2,1)S(1)} fusion(f32[256,128,128]{2,1,0:T(8,128)} %bitcast.24, f32[256,128]{1,0:T(8,128)S(1)} %convert_element_type.125), kind=kLoop, calls=%fused_computation.4 | loop fusion | flops 8372224 | bytes 16941056 | tf_op jit(solution)/shard_map/reduce_sum | solution.py:29
  425.8 47.7 %all-reduce.1 = bf16[128,128]{1,0:T(8,128)(2,1)S(1)} all-reduce(bf16[128,128]{1,0:T(8,128)(2,1)S(1)} %multiply_reduce_fusion), channel_id=5, replica_groups=mesh['row'=16,'col'=16] {'row'}, use_global_device_ids=true, to_apply=%region_18.0.clone | all-reduce | flops 16384 | bytes 65536
  473.5 86.2 %all-reduce.2 = (f32[128]{0:T(128)S(1)}, f32[128]{0:T(128)S(1)}) all-reduce(f32[128]{0:T(128)S(1)} %get-tuple-element.11, f32[128]{0:T(128)S(1)} %get-tuple-element.9), channel_id=1, replica_groups=mesh['row'=16,'col'=16] {'row','col'}, use_global_device_ids=true, to_apply=%region_10.0 | all-reduce | flops 256 | bytes 2048 | tf_op jit(solution)/shard_map/psum | solution.py:43
  559.7 0.6 multiply_add_fusion.4
  560.3 92.8 %all-reduce.9.cloned.1.call-done = f32[128,128]{1,0:T(8,128)} async-done(((f32[128,128]{1,0:T(8,128)}), f32[128,128]{1,0:T(8,128)}) %all-reduce.9.cloned.1.call-update) | async-done | bytes 65552 | tf_op jit(solution)/shard_map/psum | solution.py:60
  653.2 1.5 multiply_add_fusion
  654.6 1.3 multiply_add_fusion.2
  (30 shorter events, 0.3 us)
Async XLA Ops:
  8.0 69.1 %copy-start.2 = (f32[128,128]{1,0:T(8,128)S(1)}, f32[128,128]{1,0:T(8,128)}, u32[]{:S(2)}) copy-start(f32[128,128]{1,0:T(8,128)} %param.7) | copy-start | bytes 196612
  8.0 320.1 %all-reduce.7.cloned.1.call-start = ((), (), s32[]{:S(2)}) async-start(), calls=%async_computation.3 | async-start | bytes 131072 | tf_op jit(solution)/shard_map/psum | solution.py:60
  85.2 3.2 copy-start
  94.9 258.6 %reduce-scatter.3.cloned.1.call-start = ((), (), s32[]{:S(2)}) async-start(), calls=%async_computation.2 | async-start | bytes 69632 | tf_op jit(solution)/shard_map/reduce_scatter | solution.py:52
  107.0 546.1 %all-reduce.9.cloned.1.call-start = ((), (), s32[]{:S(2)}) async-start(), calls=%async_computation.5 | async-start | bytes 131072 | tf_op jit(solution)/shard_map/psum | solution.py:60
  107.1 53.7 %copy-start.7 = (u32[256]{0:T(256)S(1)}, u32[256]{0:T(256)}, u32[]{:S(2)}) copy-start(u32[256]{0:T(256)} %constant.14) | copy-start | bytes 3076
  107.1 221.9 %copy-start.5 = (f32[8,128]{1,0:T(8,128)S(1)}, f32[8,128]{1,0:T(8,128)}, u32[]{:S(2)}) copy-start(f32[8,128]{1,0:T(8,128)} %param.6) | copy-start | bytes 12292
  107.1 246.4 %copy-start.4 = (f32[16,128]{1,0:T(8,128)S(1)}, f32[16,128]{1,0:T(8,128)}, u32[]{:S(2)}) copy-start(f32[16,128]{1,0:T(8,128)} %param.5) | copy-start | bytes 24580
  396.7 3.2 copy-start.1
  418.4 236.2 %reduce-scatter.5.cloned.1.call-start = ((), (), s32[]{:S(2)}) async-start(), calls=%async_computation.4 | async-start | bytes 69632 | tf_op jit(solution)/shard_map/reduce_scatter | solution.py:52
  418.5 234.7 %copy-start.3 = (f32[128,128]{1,0:T(8,128)S(1)}, f32[128,128]{1,0:T(8,128)}, u32[]{:S(2)}) copy-start(f32[128,128]{1,0:T(8,128)} %all-reduce.7.cloned.1.call-done) | copy-start | bytes 196612
  418.5 236.1 %copy-start.6 = (bf16[16,128]{1,0:T(8,128)(2,1)S(1)}, bf16[16,128]{1,0:T(8,128)(2,1)}, u32[]{:S(2)}) copy-start(bf16[16,128]{1,0:T(8,128)(2,1)} %reduce-scatter.3.cloned.1.call-done) | copy-start | bytes 12292
Sparse Core Ops, SparseCore 0:
  95.0 233.1 all-reduce.6
  418.6 234.5 all-reduce.8
Sparse Core Ops, SparseCore 1:
  107.1 58.3 reduce-scatter.2
  560.4 60.9 reduce-scatter.4
where the time goes:
time: 664 us; the launch traced here: 663 us
  blocking collectives  380 us (57%)
  waiting for transfers between devices  175 us (26%)
  matrix products  53.2 us (8%)
  other arithmetic  32.4 us (5%)
  between operations  16.3 us (2%)
  local copies, waits for them, and re-layouts  7.04 us (1%)
    psum x2, waiting for transfers between devices, local(): grad_c = lax.psum(grad_c, ('row', 'col'))  175 us
    psum x2, blocking collectives, local(): lax.psum((column_squares(a_mine16), column_squares(b_mine16)), ('row', 'c...  171 us
    unnamed x2, blocking collectives  94 us
    all_gather x2, blocking collectives, local(): tile_a = lax.all_gather(a_mine16, 'col', axis=0, tiled=True)  60.5 us
    all_gather x2, blocking collectives, local(): tile_b = lax.all_gather(b_mine16, 'row', axis=0, tiled=True)  54.7 us
    dot_general x2, matrix products, local_terms(): jnp.dot(resid, c16, preferred_element_type=jnp.float32)  24.1 us
    dot_general x2, matrix products, local_terms(): model = jnp.dot(pairs, c16.T, preferred_element_type=jnp.float32)  16.2 us
    reduce_sum x2, other arithmetic, local_terms(): grad_b = jnp.sum(along * tile_a.astype(jnp.float32)[:, None, :], axis=0)  14.7 us
  transfers between devices with their start and end apart: 4, of which 2 were waited for; matrix products, arithmetic and copies ran while one was open for 5% of the time, Pallas kernels for 0%

commit v1 on v0

v1 whole, which is shorter than its diff:
```python
import jax
import jax.numpy as jnp
from jax import lax
from jax.experimental import pallas as pl
from jax.experimental.pallas import tpu as pltpu
from jax.sharding import PartitionSpec as P

STEPS = 2
N = 16
damping = 0.9
scaling = 0.25
epsilon = 1e-06

MESH = pl.DeviceIdType.MESH
bf16, f32 = jnp.bfloat16, jnp.float32
GC_UNROLL = 64
Z_UNROLL = 64
CHUNKS = 8


def peer_copy(axis, peer, src, dst, ssem, rsem):
    return pltpu.make_async_remote_copy(
        src_ref=src, dst_ref=dst, send_sem=ssem, recv_sem=rsem, device_id={axis: peer}, device_id_type=MESH
    )


def send_all(axis, me, src_of, dst, ssem, rsem):
    def body(d, carry):
        p = lax.rem(me + d, N)
        peer_copy(axis, p, src_of(p), dst.at[me], ssem.at[p], rsem.at[me]).start()
        return carry

    lax.fori_loop(1, N, body, 0)


def recv_all(axis, me, dst, ssem, rsem):
    def body(d, carry):
        p = lax.rem(me + d, N)
        peer_copy(axis, p, dst.at[p], dst.at[p], ssem.at[p], rsem.at[p]).wait_recv()
        return carry

    lax.fori_loop(1, N, body, 0)


def drain_all(axis, me, src_of, dst, ssem, rsem):
    def body(d, carry):
        p = lax.rem(me + d, N)
        peer_copy(axis, p, src_of(p), dst.at[me], ssem.at[p], rsem.at[me]).wait_send()
        return carry

    lax.fori_loop(1, N, body, 0)


def split_dot(x16, g):
    hi = g.astype(bf16)
    lo = (g - hi.astype(f32)).astype(bf16)
    return jnp.dot(x16, hi, preferred_element_type=f32) + jnp.dot(x16, lo, preferred_element_type=f32)


def third_mode(tv, ta_t, tb_t):
    rows_i, rows_j, depth = tv.shape
    rank = tb_t.shape[0]
    unroll = GC_UNROLL

    def body(ib, acc):
        at = ta_t[ib]
        bt = tb_t[...]
        pairs = jnp.concatenate(
            [bt * jnp.broadcast_to(at[:, u : u + 1], (rank, rows_j)) for u in range(unroll)], axis=1
        )
        block = tv[pl.ds(ib * unroll, unroll)].reshape(unroll * rows_j, depth)
        return acc + jnp.dot(pairs, block, preferred_element_type=f32)

    return lax.fori_loop(0, rows_i // unroll, body, jnp.zeros((rank, depth), f32))


def first_modes(tv, ta32, tb32, c16, ga):
    rows_i, rows_j, depth = tv.shape
    rank = c16.shape[1]
    unroll = Z_UNROLL

    def body(ib, gb):
        b = tb32[...]
        block = tv[pl.ds(ib * unroll, unroll)].reshape(unroll * rows_j, depth)
        along = jnp.dot(block, c16[...], preferred_element_type=f32)
        rows = []
        for u in range(unroll):
            z = along[u * rows_j : (u + 1) * rows_j]
            rows.append(jnp.sum(z * b, axis=0, keepdims=True))
            gb = gb + z * ta32[pl.ds(ib * unroll + u, 1), :]
        ga[pl.ds(ib * unroll, unroll), :] = jnp.concatenate(rows, axis=0)
        return gb

    return lax.fori_loop(0, rows_i // unroll, body, jnp.zeros((rows_j, rank), f32))


def kernel(
    t_ref, a_ref, b_ref, c_ref, oa_ref, ob_ref, oc_ref,
    tv, ta, tb, ta32, tb32, ta_t, tb_t, c16, ga,
    a16, b16, sa, sb, ra, rb, na_s, nb_s, na_r, nb_r, c1s, c1r, c2s, c2r, c3s, c3r,
    tsem, ssem, rsem,
):
    row, col = lax.axis_index("row"), lax.axis_index("col")
    rows_i, rows_j, depth = tv.shape
    rank = tb_t.shape[0]
    part = rows_i // CHUNKS

    def chunk(i):
        view = pl.ds(i * part, part)
        return pltpu.make_async_copy(t_ref.at[view], tv.at[view], tsem.at[i])

    for i in range(CHUNKS):
        chunk(i).start()

    barrier = pltpu.get_barrier_semaphore()

    def greet(d, carry):
        pl.semaphore_signal(barrier, inc=1, device_id={"row": lax.rem(row + d, N)}, device_id_type=MESH)
        pl.semaphore_signal(barrier, inc=1, device_id={"col": lax.rem(col + d, N)}, device_id_type=MESH)
        return carry

    lax.fori_loop(1, N, greet, 0)

    own_a, own_b = a_ref[...], b_ref[...]
    own_c = c_ref[pl.ds(pl.multiple_of(col * 8, 8), 8), :]
    third = c_ref[...]
    sent = []

    def exchange(axis, kind, src_of, dst):
        me = row if axis == "row" else col
        args = (axis, me, src_of, dst, ssem.at[kind], rsem.at[kind])
        send_all(*args)
        sent.append(args)

    def arrive(axis, kind, dst):
        me = row if axis == "row" else col
        recv_all(axis, me, dst, ssem.at[kind], rsem.at[kind])

    def gather(step, own_a, own_b):
        a16[step] = own_a.astype(bf16)
        b16[step] = own_b.astype(bf16)
        ta[step, col] = own_a.astype(bf16)
        tb[step, row] = own_b.astype(bf16)
        exchange("col", step * 9 + 0, lambda p: a16.at[step], ta.at[step])
        exchange("row", step * 9 + 1, lambda p: b16.at[step], tb.at[step])

    pl.semaphore_wait(barrier, 2 * (N - 1))
    gather(0, own_a, own_b)

    for step in range(STEPS):
        k0 = step * 9
        arrive("col", k0 + 0, ta.at[step])
        arrive("row", k0 + 1, tb.at[step])
        at16 = ta[step].reshape(rows_i, rank)
        b_full = tb[step].astype(f32).reshape(rows_j, rank)
        bt16 = b_full.astype(bf16)
        a_full = at16.astype(f32)
        ta32[...] = a_full
        tb32[...] = b_full
        part_na = jnp.sum(a_full * a_full, axis=0, keepdims=True)
        part_nb = jnp.sum(b_full * b_full, axis=0, keepdims=True)
        na_s[step] = part_na
        nb_s[step] = part_nb
        na_r[step, row] = part_na
        nb_r[step, col] = part_nb
        exchange("row", k0 + 2, lambda p: na_s.at[step], na_r.at[step])
        exchange("col", k0 + 3, lambda p: nb_s.at[step], nb_r.at[step])

        flip_a = a_full.T
        flip_b = b_full.T.astype(bf16)
        tb_t[...] = flip_b
        for ib in range(rows_i // GC_UNROLL):
            lane = ib * GC_UNROLL
            half = flip_a[:, lane // 128 * 128 : lane // 128 * 128 + 128]
            if lane % 128:
                half = pltpu.roll(half, 128 - lane % 128, 1)
            ta_t[ib] = half.astype(bf16)
        gram_a = jnp.dot(flip_a.astype(bf16), at16, preferred_element_type=f32)
        gram_b = jnp.dot(flip_b, bt16, preferred_element_type=f32)

        if step == 0:
            for i in range(CHUNKS):
                chunk(i).wait()
        gc_t = third_mode(tv, ta_t, tb_t)
        if step:
            arrive("col", k0 - 9 + 8, c3r.at[step - 1])
            third = c3r[step - 1].reshape(depth, rank)
        third16 = third.astype(bf16)
        c16[...] = third16
        c32 = third16.astype(f32)
        gram_c = jnp.dot(c32.T.astype(bf16), third16, preferred_element_type=f32)
        norm_c = jnp.sum(c32 * c32, axis=0, keepdims=True)

        gc = gc_t.T - split_dot(third16, gram_a * gram_b)
        c1s[step] = gc.reshape(N, 8, rank)
        c1r[step, col] = c1s[step, col]
        exchange("col", k0 + 4, lambda p: c1s.at[step, p], c1r.at[step])

        gb = first_modes(tv, ta32, tb32, c16, ga)
        gb = gb - split_dot(bt16, gram_a * gram_c)
        grad_a = ga[...] - split_dot(at16, gram_b * gram_c)
        sa[step] = grad_a.astype(bf16).reshape(N, 16, rank)
        sb[step] = gb.reshape(N, 8, rank).astype(bf16)
        ra[step, col] = sa[step, col]
        rb[step, row] = sb[step, row]
        exchange("col", k0 + 5, lambda p: sa.at[step, p], ra.at[step])
        exchange("row", k0 + 6, lambda p: sb.at[step, p], rb.at[step])

        arrive("col", k0 + 4, c1r.at[step])
        piece = jnp.sum(c1r[step], axis=0)
        c2s[step] = piece
        c2r[step, row] = piece
        exchange("row", k0 + 7, lambda p: c2s.at[step], c2r.at[step])

        arrive("row", k0 + 2, na_r.at[step])
        arrive("col", k0 + 3, nb_r.at[step])
        norm_a = jnp.sum(na_r[step], axis=0)
        norm_b = jnp.sum(nb_r[step], axis=0)
        step_a = scaling / (norm_b * norm_c + epsilon)
        step_b = scaling / (norm_a * norm_c + epsilon)
        step_c = scaling / (norm_a * norm_b + epsilon)

        arrive("col", k0 + 5, ra.at[step])
        arrive("row", k0 + 6, rb.at[step])
        own_a = damping * own_a + step_a * jnp.sum(ra[step].astype(f32), axis=0)
        own_b = damping * own_b + step_b * jnp.sum(rb[step].astype(f32), axis=0)
        if step + 1 < STEPS:
            gather(step + 1, own_a, own_b)
        else:
            oa_ref[...] = own_a
            ob_ref[...] = own_b

        arrive("row", k0 + 7, c2r.at[step])
        own_c = damping * own_c + step_c * jnp.sum(c2r[step], axis=0)
        c3s[step] = own_c
        c3r[step, col] = own_c
        exchange("col", k0 + 8, lambda p: c3s.at[step], c3r.at[step])

    arrive("col", 9 * (STEPS - 1) + 8, c3r.at[STEPS - 1])
    oc_ref[...] = c3r[STEPS - 1].reshape(depth, rank)
    for args in sent:
        drain_all(*args)


def local(tensor, factor_a, factor_b, factor_c):
    rows_i, rows_j, depth = tensor.shape
    mine_a, rank = factor_a.shape
    mine_b = factor_b.shape[0]
    vmem = pl.BlockSpec(memory_space=pltpu.VMEM)
    V, S = pltpu.VMEM, STEPS
    return pl.pallas_call(
        kernel,
        out_shape=[jax.ShapeDtypeStruct(x.shape, f32) for x in (factor_a, factor_b, factor_c)],
        in_specs=[pl.BlockSpec(memory_space=pl.ANY), vmem, vmem, vmem],
        out_specs=[vmem, vmem, vmem],
        scratch_shapes=[
            V((rows_i, rows_j, depth), bf16),
            V((S, N, mine_a, rank), bf16),
            V((S, N, mine_b, rank), bf16),
            V((rows_i, rank), f32),
            V((rows_j, rank), f32),
            V((rows_i // GC_UNROLL, rank, 128), bf16),
            V((rank, rows_j), bf16),
            V((depth, rank), bf16),
            V((rows_i, rank), f32),
            V((S, mine_a, rank), bf16),
            V((S, mine_b, rank), bf16),
            V((S, N, mine_a, rank), bf16),
            V((S, N, mine_b, rank), bf16),
            V((S, N, mine_a, rank), bf16),
            V((S, N, mine_b, rank), bf16),
            V((S, 1, rank), f32),
            V((S, 1, rank), f32),
            V((S, N, 1, rank), f32),
            V((S, N, 1, rank), f32),
            V((S, N, 8, rank), f32),
            V((S, N, 8, rank), f32),
            V((S, 8, rank), f32),
            V((S, N, 8, rank), f32),
            V((S, 8, rank), f32),
            V((S, N, 8, rank), f32),
            pltpu.SemaphoreType.DMA((CHUNKS,)),
            pltpu.SemaphoreType.DMA((9 * S, N)),
            pltpu.SemaphoreType.DMA((9 * S, N)),
        ],
        compiler_params=pltpu.CompilerParams(collective_id=0, has_side_effects=True),
    )(tensor, factor_a, factor_b, factor_c)


def solution(mesh):
    return jax.shard_map(
        local,
        mesh=mesh,
        in_specs=(P("row", "col", None), P(("row", "col"), None), P(("col", "row"), None), P()),
        out_specs=(P(("row", "col"), None), P(("col", "row"), None), P()),
        check_vma=False,
    )
```

time: 664 us -> 73.6 us (0.11)
  blocking collectives: 380 us -> 0 us
  waiting for transfers between devices: 175 us -> 0 us
  Pallas kernels: 0 us -> 68.6 us
  matrix products: 53.2 us -> 0 us
  other arithmetic: 32.4 us -> 0 us
  between operations: 16.3 us -> 0.64 us
    psum x2 -> x0, waiting for transfers between devices: 175 us -> none  [local(): grad_c = lax.psum(grad_c, ('row', 'col'))]
    psum x2 -> x0, blocking collectives: 171 us -> none  [local(): lax.psum((column_squares(a_mine16), column_squares(b_mine16)), ('row', 'c...]
    all_gather x4 -> x0, blocking collectives: 115 us -> none  [the longest x2 60.5 us: local(): tile_a = lax.all_gather(a_mine16, 'col', axis=0, tiled=True)]
    unnamed x2 -> x0, blocking collectives: 94 us -> none
    pallas_call x0 -> x1, Pallas kernels: none -> 68.6 us  [local(): pl.pallas_call(kernel, out_shape=[jax.ShapeDtypeStruct(x.shape, f32) for...]
    dot_general x6 -> x0, matrix products: 53.2 us -> none  [the longest x2 24.1 us: local_terms(): jnp.dot(resid, c16, preferred_element_type=jnp.float32)]
    reduce_sum x7 -> x0, other arithmetic: 17.7 us -> none  [the longest x2 14.7 us: local_terms(): grad_b = jnp.sum(along * tile_a.astype(jnp.float32)[:, None, :], axis=0)]
    convert_element_type x6 -> x0, other arithmetic: 11.3 us -> none  [the longest x2 11.2 us: local_terms(): pairs = (tile_a.astype(jnp.float32)[:, None, :] * tile_b.astype(jnp.float...]
  transfers between devices with their start and end apart: 4 -> 0, of which waited for: 2 -> 0; matrix products, arithmetic and copies ran while one was open for 5% -> 0% of each run, Pallas kernels for 0% -> 0%
where the time goes in v1:
time: 73.6 us; the launch traced here: 73.3 us
  Pallas kernels  68.6 us (93%)
  local copies, waits for them, and re-layouts  4.04 us (5%)
    pallas_call x1, Pallas kernels, local(): pl.pallas_call(kernel, out_shape=[jax.ShapeDtypeStruct(x.shape, f32) for...  68.6 us
    unnamed x3, local copies, waits for them, and re-layouts  4.04 us

profile of v1, /device:TPU:1, one launch (start us, length us, event | category | flops | bytes accessed | tf_op | source)
XLA Modules:
  0.0 73.3 jit_solution(3397998513522659029)
XLA Ops:
  0.6 68.6 %shard_map.67 = (f32[16,128]{1,0:T(8,128)}, f32[8,128]{1,0:T(8,128)}, f32[128,128]{1,0:T(8,128)}) custom-call(bf16[256,128,128]{2,1,0:T(8,128)(2,1)} %t_ref.1, f32[16,128]{1,0:T(8,128)} %a_ref.1, f32[8,128]{1,0:T(8,128)} %b_ref.1, f32[128,128]{1,0:T(8,128)} %c_ref.1), custom_call_target="tpu_custom_call" | custom-call | tf_op jit(solution)/shard_map/pallas_call | solution.py:251
  69.3 1.3 %copy.10 = f32[16,128]{1,0:T(8,128)} copy(f32[16,128]{1,0:T(8,128)} %get-tuple-element.6) | data formatting | bytes 16384
  70.6 1.3 %copy.11 = f32[8,128]{1,0:T(8,128)} copy(f32[8,128]{1,0:T(8,128)} %get-tuple-element.7) | data formatting | bytes 8192
  71.8 1.5 %copy.12 = f32[128,128]{1,0:T(8,128)} copy(f32[128,128]{1,0:T(8,128)} %get-tuple-element.8) | data formatting | bytes 131072

commit v2 on v0

v2 whole, which is shorter than its diff:
```python
import jax
import jax.numpy as jnp
from jax import lax
from jax.experimental import pallas as pl
from jax.experimental.pallas import tpu as pltpu
from jax.sharding import PartitionSpec as P

STEPS = 2
N = 16
Z = 8
Q = 32
damping = 0.9
scaling = 0.25
epsilon = 1e-06

MESH = pl.DeviceIdType.MESH
bf16, f32 = jnp.bfloat16, jnp.float32
UNROLL = 64
CHUNKS = 8


class Group:
    def __init__(self, size, me, device):
        self.size, self.me, self.device = size, me, device

    def each(self, act):
        def body(d, carry):
            act(lax.rem(self.me + d, self.size))
            return carry

        lax.fori_loop(1, self.size, body, 0)


def remote(group, peer, src, dst, ssem, rsem):
    return pltpu.make_async_remote_copy(
        src_ref=src, dst_ref=dst, send_sem=ssem, recv_sem=rsem, device_id=group.device(peer), device_id_type=MESH
    )


def split_dot(x16, g):
    hi = g.astype(bf16)
    lo = (g - hi.astype(f32)).astype(bf16)
    return jnp.dot(x16, hi, preferred_element_type=f32) + jnp.dot(x16, lo, preferred_element_type=f32)


def swap(tv, tt, base, count):
    for u in range(count):
        tt[base + u] = tv[base + u].T


def third_mode(tt, ta32, tb16):
    rows_i, depth, rows_j = tt.shape
    rank = ta32.shape[1]

    def body(ib, gc):
        block = tt[pl.ds(ib * UNROLL, UNROLL)].reshape(UNROLL * depth, rows_j)
        along = jnp.dot(block, tb16[...], preferred_element_type=f32)
        for u in range(UNROLL):
            gc = gc + along[u * depth : (u + 1) * depth] * ta32[pl.ds(ib * UNROLL + u, 1), :]
        return gc

    return lax.fori_loop(0, rows_i // UNROLL, body, jnp.zeros((depth, rank), f32))


def first_modes(tv, ta32, tb32, c16, ga):
    rows_i, rows_j, depth = tv.shape
    rank = c16.shape[1]

    def body(ib, gb):
        b = tb32[...]
        block = tv[pl.ds(ib * UNROLL, UNROLL)].reshape(UNROLL * rows_j, depth)
        along = jnp.dot(block, c16[...], preferred_element_type=f32)
        rows = []
        for u in range(UNROLL):
            z = along[u * rows_j : (u + 1) * rows_j]
            rows.append(jnp.sum(z * b, axis=0, keepdims=True))
            gb = gb + z * ta32[pl.ds(ib * UNROLL + u, 1), :]
        ga[pl.ds(ib * UNROLL, UNROLL), :] = jnp.concatenate(rows, axis=0)
        return gb

    return lax.fori_loop(0, rows_i // UNROLL, body, jnp.zeros((rows_j, rank), f32))


AG_A, AG_B, NORM_A, NORM_B, RS_A, RS_B = range(6)
PLANE_RS, PLANE_AG = range(2)


def kernel(
    t_ref, a_ref, b_ref, c_ref, oa_ref, ob_ref, oc_ref,
    tv, tt, ta, tb, ta32, tb32, tb16, c16, cq, ga,
    a16, b16, sa, sb, ra, rb, na_s, nb_s, na_r, nb_r, c1s, c1r, c2s, c2r, c3s, c3r,
    tsem, ssem, rsem, plane_ssem, plane_rsem, line_ssem, line_rsem,
):
    row, col = lax.axis_index("row"), lax.axis_index("col")
    x_lo, z = lax.div(row, Z), lax.rem(row, Z)
    q = x_lo * N + col
    rows_i, rows_j, depth = tv.shape
    rank = c16.shape[1]
    part = rows_i // CHUNKS
    rows = Group(N, row, lambda p: (p, col))
    cols = Group(N, col, lambda p: (row, p))
    plane = Group(Q, q, lambda p: (lax.div(p, N) * Z + z, lax.rem(p, N)))
    line = Group(Z, z, lambda p: (x_lo * Z + p, col))

    def chunk(i):
        view = pl.ds(i * part, part)
        return pltpu.make_async_copy(t_ref.at[view], tv.at[view], tsem.at[i])

    for i in range(CHUNKS):
        chunk(i).start()

    barrier = pltpu.get_barrier_semaphore()

    def greet(group):
        group.each(
            lambda p: pl.semaphore_signal(barrier, inc=1, device_id=group.device(p), device_id_type=MESH)
        )

    greet(rows)
    greet(plane)

    sent = []

    def others(group, dst, ss, rs):
        view = dst.at[pl.ds(0, group.size - 1)]
        return remote(group, group.me, view, view, ss, rs)

    def send(group, src_of, dst, ss, rs):
        group.each(lambda p: remote(group, p, src_of(p), dst.at[group.me], ss, rs).start())
        sent.append((group, dst, ss, rs))

    def arrive(group, dst, ss, rs):
        others(group, dst, ss, rs).wait_recv()

    def sems(step, kind):
        return ssem.at[step * 6 + kind], rsem.at[step * 6 + kind]

    def plane_sems(step, kind):
        return plane_ssem.at[step * 2 + kind], plane_rsem.at[step * 2 + kind]

    def line_sems(step):
        return line_ssem.at[step], line_rsem.at[step]

    def gather_factors(step, own_a, own_b):
        b16[step] = own_b.astype(bf16)
        a16[step] = own_a.astype(bf16)
        send(rows, lambda p: b16.at[step], tb.at[step], *sems(step, AG_B))
        send(cols, lambda p: a16.at[step], ta.at[step], *sems(step, AG_A))
        tb[step, row] = own_b.astype(bf16)
        ta[step, col] = own_a.astype(bf16)

    def take_third(third):
        third16 = third.astype(bf16)
        c16[...] = third16
        c32 = third16.astype(f32)
        gram = jnp.dot(c32.T.astype(bf16), third16, preferred_element_type=f32)
        return third16, gram, jnp.sum(c32 * c32, axis=0, keepdims=True)

    def take_factors(step):
        arrive(cols, ta.at[step], *sems(step, AG_A))
        arrive(rows, tb.at[step], *sems(step, AG_B))
        a_full = ta[step].reshape(rows_i, rank).astype(f32)
        b_full = tb[step].astype(f32).reshape(rows_j, rank)
        ta32[...] = a_full
        tb32[...] = b_full
        tb16[...] = b_full.astype(bf16)
        part_na = jnp.sum(a_full * a_full, axis=0, keepdims=True)
        part_nb = jnp.sum(b_full * b_full, axis=0, keepdims=True)
        na_s[step] = part_na
        nb_s[step] = part_nb
        na_r[step, row] = part_na
        nb_r[step, col] = part_nb
        send(rows, lambda p: na_s.at[step], na_r.at[step], *sems(step, NORM_A))
        send(cols, lambda p: nb_s.at[step], nb_r.at[step], *sems(step, NORM_B))

    def grams(step):
        gram_a = jnp.dot(ta32[...].T.astype(bf16), ta[step].reshape(rows_i, rank), preferred_element_type=f32)
        gram_b = jnp.dot(tb32[...].T.astype(bf16), tb16[...], preferred_element_type=f32)
        return gram_a, gram_b

    def do_first_modes(step, gram_a, gram_b, gram_c):
        gb = first_modes(tv, ta32, tb32, c16, ga)
        gb = gb - split_dot(tb16[...], gram_a * gram_c)
        grad_a = ga[...] - split_dot(ta[step].reshape(rows_i, rank), gram_b * gram_c)
        sb[step] = gb.reshape(N, 8, rank).astype(bf16)
        sa[step] = grad_a.astype(bf16).reshape(N, 16, rank)
        send(rows, lambda p: sb.at[step, p], rb.at[step], *sems(step, RS_B))
        send(cols, lambda p: sa.at[step, p], ra.at[step], *sems(step, RS_A))
        rb[step, row] = sb[step, row]
        ra[step, col] = sa[step, col]

    def scatter_third(step, gc, third16, gram_a, gram_b):
        gc = gc - split_dot(third16, gram_a * gram_b)
        c1s[step] = gc.reshape(Q, 4, rank)
        send(plane, lambda p: c1s.at[step, p], c1r.at[step], *plane_sems(step, PLANE_RS))
        c1r[step, q] = c1s[step, q]

    def line_third(step):
        arrive(plane, c1r.at[step], *plane_sems(step, PLANE_RS))
        piece = jnp.sum(c1r[step], axis=0)
        c2s[step] = piece
        send(line, lambda p: c2s.at[step], c2r.at[step], *line_sems(step))
        c2r[step, z] = piece

    def gather_third(step, own_c, step_c):
        arrive(line, c2r.at[step], *line_sems(step))
        own_c = damping * own_c + step_c * jnp.sum(c2r[step], axis=0)
        c3s[step] = own_c
        send(plane, lambda p: c3s.at[step], c3r.at[step], *plane_sems(step, PLANE_AG))
        c3r[step, q] = own_c
        return own_c

    def whole_third(step):
        arrive(plane, c3r.at[step], *plane_sems(step, PLANE_AG))
        return c3r[step].reshape(depth, rank)

    def sizes(step, norm_c):
        arrive(rows, na_r.at[step], *sems(step, NORM_A))
        arrive(cols, nb_r.at[step], *sems(step, NORM_B))
        norm_a = jnp.sum(na_r[step], axis=0)
        norm_b = jnp.sum(nb_r[step], axis=0)
        return (
            scaling / (norm_b * norm_c + epsilon),
            scaling / (norm_a * norm_c + epsilon),
            scaling / (norm_a * norm_b + epsilon),
        )

    def update_first(step, own_a, own_b, step_a, step_b):
        arrive(rows, rb.at[step], *sems(step, RS_B))
        arrive(cols, ra.at[step], *sems(step, RS_A))
        own_a = damping * own_a + step_a * jnp.sum(ra[step].astype(f32), axis=0)
        own_b = damping * own_b + step_b * jnp.sum(rb[step].astype(f32), axis=0)
        return own_a, own_b

    own_a, own_b = a_ref[...], b_ref[...]
    third16, gram_c, norm_c = take_third(c_ref[...])
    cq[...] = c_ref[...].reshape(Q, 4, rank)
    own_c = cq[q]
    pl.semaphore_wait(barrier, N - 1 + Q - 1)
    gather_factors(0, own_a, own_b)

    def turn(i, carry):
        chunk(i).wait()
        swap(tv, tt, i * part, part)
        return carry

    lax.fori_loop(0, CHUNKS, turn, 0)

    take_factors(0)
    gram_a, gram_b = grams(0)
    do_first_modes(0, gram_a, gram_b, gram_c)
    gc = third_mode(tt, ta32, tb16)
    scatter_third(0, gc, third16, gram_a, gram_b)
    step_a, step_b, step_c = sizes(0, norm_c)
    own_a, own_b = update_first(0, own_a, own_b, step_a, step_b)
    gather_factors(1, own_a, own_b)
    line_third(0)

    take_factors(1)
    gram_a, gram_b = grams(1)
    own_c = gather_third(0, own_c, step_c)
    gc = third_mode(tt, ta32, tb16)
    third16, gram_c, norm_c = take_third(whole_third(0))
    scatter_third(1, gc, third16, gram_a, gram_b)
    do_first_modes(1, gram_a, gram_b, gram_c)
    line_third(1)
    step_a, step_b, step_c = sizes(1, norm_c)
    own_a, own_b = update_first(1, own_a, own_b, step_a, step_b)
    oa_ref[...] = own_a
    ob_ref[...] = own_b
    gather_third(1, own_c, step_c)
    oc_ref[...] = whole_third(1)

    for group, dst, ss, rs in sent:
        others(group, dst, ss, rs).wait_send()


def hand_over(a_ref, b_ref, c_ref, oa_ref, ob_ref, oc_ref):
    oa_ref[...] = a_ref[...]
    ob_ref[...] = b_ref[...]
    oc_ref[...] = c_ref[...]


def local(tensor, factor_a, factor_b, factor_c):
    rows_i, rows_j, depth = tensor.shape
    mine_a, rank = factor_a.shape
    mine_b = factor_b.shape[0]
    vmem = pl.BlockSpec(memory_space=pltpu.VMEM)
    V, S, D = pltpu.VMEM, STEPS, pltpu.SemaphoreType.DMA
    outs = pl.pallas_call(
        kernel,
        out_shape=[jax.ShapeDtypeStruct(x.shape, f32) for x in (factor_a, factor_b, factor_c)],
        in_specs=[pl.BlockSpec(memory_space=pl.ANY), vmem, vmem, vmem],
        out_specs=[vmem, vmem, vmem],
        scratch_shapes=[
            V((rows_i, rows_j, depth), bf16),
            V((rows_i, depth, rows_j), bf16),
            V((S, N, mine_a, rank), bf16),
            V((S, N, mine_b, rank), bf16),
            V((rows_i, rank), f32),
            V((rows_j, rank), f32),
            V((rows_j, rank), bf16),
            V((depth, rank), bf16),
            V((Q, 4, rank), f32),
            V((rows_i, rank), f32),
            V((S, mine_a, rank), bf16),
            V((S, mine_b, rank), bf16),
            V((S, N, mine_a, rank), bf16),
            V((S, N, mine_b, rank), bf16),
            V((S, N, mine_a, rank), bf16),
            V((S, N, mine_b, rank), bf16),
            V((S, 1, rank), f32),
            V((S, 1, rank), f32),
            V((S, N, 1, rank), f32),
            V((S, N, 1, rank), f32),
            V((S, Q, 4, rank), f32),
            V((S, Q, 4, rank), f32),
            V((S, 4, rank), f32),
            V((S, Z, 4, rank), f32),
            V((S, 4, rank), f32),
            V((S, Q, 4, rank), f32),
            D((CHUNKS,)),
            D((6 * S,)),
            D((6 * S,)),
            D((2 * S,)),
            D((2 * S,)),
            D((S,)),
            D((S,)),
        ],
        compiler_params=pltpu.CompilerParams(collective_id=0, has_side_effects=True),
    )(tensor, factor_a, factor_b, factor_c)
    return pl.pallas_call(
        hand_over,
        out_shape=[jax.ShapeDtypeStruct(x.shape, f32) for x in (factor_a, factor_b, factor_c)],
        in_specs=[vmem, vmem, vmem],
        out_specs=[vmem, vmem, vmem],
    )(*outs)


def solution(mesh):
    return jax.shard_map(
        local,
        mesh=mesh,
        in_specs=(P("row", "col", None), P(("row", "col"), None), P(("col", "row"), None), P()),
        out_specs=(P(("row", "col"), None), P(("col", "row"), None), P()),
        check_vma=False,
    )
```

time: 664 us -> 57.6 us (0.09)
  blocking collectives: 380 us -> 0 us
  waiting for transfers between devices: 175 us -> 0 us
  Pallas kernels: 0 us -> 56.8 us
  matrix products: 53.2 us -> 0 us
  other arithmetic: 32.4 us -> 0 us
  between operations: 16.3 us -> 0.64 us
  local copies, waits for them, and re-layouts: 7.04 us -> 0 us
    psum x2 -> x0, waiting for transfers between devices: 175 us -> none  [local(): grad_c = lax.psum(grad_c, ('row', 'col'))]
    psum x2 -> x0, blocking collectives: 171 us -> none  [local(): lax.psum((column_squares(a_mine16), column_squares(b_mine16)), ('row', 'c...]
    all_gather x4 -> x0, blocking collectives: 115 us -> none  [the longest x2 60.5 us: local(): tile_a = lax.all_gather(a_mine16, 'col', axis=0, tiled=True)]
    unnamed x2 -> x0, blocking collectives: 94 us -> none
    pallas_call x0 -> x2, Pallas kernels: none -> 56.8 us  [the longest x1 55.3 us: local(): pl.pallas_call(kernel, out_shape=[jax.ShapeDtypeStruct(x.shape, f32) for...]
    dot_general x6 -> x0, matrix products: 53.2 us -> none  [the longest x2 24.1 us: local_terms(): jnp.dot(resid, c16, preferred_element_type=jnp.float32)]
    reduce_sum x7 -> x0, other arithmetic: 17.7 us -> none  [the longest x2 14.7 us: local_terms(): grad_b = jnp.sum(along * tile_a.astype(jnp.float32)[:, None, :], axis=0)]
    convert_element_type x6 -> x0, other arithmetic: 11.3 us -> none  [the longest x2 11.2 us: local_terms(): pairs = (tile_a.astype(jnp.float32)[:, None, :] * tile_b.astype(jnp.float...]
  transfers between devices with their start and end apart: 4 -> 0, of which waited for: 2 -> 0; matrix products, arithmetic and copies ran while one was open for 5% -> 0% of each run, Pallas kernels for 0% -> 0%
where the time goes in v2:
time: 57.6 us; the launch traced here: 57.5 us
  Pallas kernels  56.8 us (99%)
  between operations  0.64 us (1%)
    pallas_call x1, Pallas kernels, local(): pl.pallas_call(kernel, out_shape=[jax.ShapeDtypeStruct(x.shape, f32) for...  55.3 us
    pallas_call x1, Pallas kernels, local(): pl.pallas_call(hand_over, out_shape=[jax.ShapeDtypeStruct(x.shape, f32) f...  1.5 us

profile of v2, /device:TPU:1, one launch (start us, length us, event | category | flops | bytes accessed | tf_op | source)
XLA Modules:
  0.0 57.5 jit_solution(16127873536714385935)
XLA Ops:
  0.6 55.3 %shard_map.67 = (f32[16,128]{1,0:T(8,128)}, f32[8,128]{1,0:T(8,128)}, f32[128,128]{1,0:T(8,128)}) custom-call(bf16[256,128,128]{2,1,0:T(8,128)(2,1)} %t_ref.1, f32[16,128]{1,0:T(8,128)} %a_ref.1, f32[8,128]{1,0:T(8,128)} %b_ref.1, f32[128,128]{1,0:T(8,128)} %c_ref.1), custom_call_target="tpu_custom_call" | custom-call | tf_op jit(solution)/shard_map/pallas_call | solution.py:290
  56.0 1.5 %shard_map.68 = (f32[16,128]{1,0:T(8,128)}, f32[8,128]{1,0:T(8,128)}, f32[128,128]{1,0:T(8,128)}) custom-call(f32[16,128]{1,0:T(8,128)} %get-tuple-element.6.a_ref, f32[8,128]{1,0:T(8,128)} %get-tuple-element.7.b_ref, f32[128,128]{1,0:T(8,128)} %get-tuple-element.8.c_ref), custom_call_target="tpu_custom_call" | custom-call | tf_op jit(solution)/shard_map/pallas_call | solution.py:332

commit v3 on v2

--- a/solution.py
+++ b/solution.py
@@ -15,20 +15,19 @@
 
 MESH = pl.DeviceIdType.MESH
 bf16, f32 = jnp.bfloat16, jnp.float32
-UNROLL = 64
+UNROLL = 128
 CHUNKS = 8
 
 
 class Group:
-    def __init__(self, size, me, device):
+    def __init__(self, size, me, device, ring, unit):
         self.size, self.me, self.device = size, me, device
+        near = lambda d: min(d // unit % ring, -(d // unit) % ring)
+        self.offsets = sorted(range(1, size), key=lambda d: -near(d))
 
     def each(self, act):
-        def body(d, carry):
+        for d in self.offsets:
             act(lax.rem(self.me + d, self.size))
-            return carry
-
-        lax.fori_loop(1, self.size, body, 0)
 
 
 def remote(group, peer, src, dst, ssem, rsem):
@@ -37,9 +36,13 @@
     )
 
 
-def split_dot(x16, g):
+def split(g):
     hi = g.astype(bf16)
-    lo = (g - hi.astype(f32)).astype(bf16)
+    return hi, (g - hi.astype(f32)).astype(bf16)
+
+
+def split_dot(x16, parts):
+    hi, lo = parts
     return jnp.dot(x16, hi, preferred_element_type=f32) + jnp.dot(x16, lo, preferred_element_type=f32)
 
 
@@ -97,10 +100,10 @@
     rows_i, rows_j, depth = tv.shape
     rank = c16.shape[1]
     part = rows_i // CHUNKS
-    rows = Group(N, row, lambda p: (p, col))
-    cols = Group(N, col, lambda p: (row, p))
-    plane = Group(Q, q, lambda p: (lax.div(p, N) * Z + z, lax.rem(p, N)))
-    line = Group(Z, z, lambda p: (x_lo * Z + p, col))
+    rows = Group(N, row, lambda p: (p, col), Z, 1)
+    cols = Group(N, col, lambda p: (row, p), 4, 2)
+    plane = Group(Q, q, lambda p: (lax.div(p, N) * Z + z, lax.rem(p, N)), 4, 2)
+    line = Group(Z, z, lambda p: (x_lo * Z + p, col), Z, 1)
 
     def chunk(i):
         view = pl.ds(i * part, part)
@@ -149,12 +152,11 @@
         tb[step, row] = own_b.astype(bf16)
         ta[step, col] = own_a.astype(bf16)
 
-    def take_third(third):
-        third16 = third.astype(bf16)
+    def take_third(third16):
         c16[...] = third16
         c32 = third16.astype(f32)
         gram = jnp.dot(c32.T.astype(bf16), third16, preferred_element_type=f32)
-        return third16, gram, jnp.sum(c32 * c32, axis=0, keepdims=True)
+        return gram, jnp.sum(c32 * c32, axis=0, keepdims=True)
 
     def take_factors(step):
         arrive(cols, ta.at[step], *sems(step, AG_A))
@@ -164,6 +166,9 @@
         ta32[...] = a_full
         tb32[...] = b_full
         tb16[...] = b_full.astype(bf16)
+
+    def send_norms(step):
+        a_full, b_full = ta32[...], tb32[...]
         part_na = jnp.sum(a_full * a_full, axis=0, keepdims=True)
         part_nb = jnp.sum(b_full * b_full, axis=0, keepdims=True)
         na_s[step] = part_na
@@ -180,8 +185,8 @@
 
     def do_first_modes(step, gram_a, gram_b, gram_c):
         gb = first_modes(tv, ta32, tb32, c16, ga)
-        gb = gb - split_dot(tb16[...], gram_a * gram_c)
-        grad_a = ga[...] - split_dot(ta[step].reshape(rows_i, rank), gram_b * gram_c)
+        gb = gb - split_dot(tb16[...], split(gram_a * gram_c))
+        grad_a = ga[...] - split_dot(ta[step].reshape(rows_i, rank), split(gram_b * gram_c))
         sb[step] = gb.reshape(N, 8, rank).astype(bf16)
         sa[step] = grad_a.astype(bf16).reshape(N, 16, rank)
         send(rows, lambda p: sb.at[step, p], rb.at[step], *sems(step, RS_B))
@@ -189,8 +194,8 @@
         rb[step, row] = sb[step, row]
         ra[step, col] = sa[step, col]
 
-    def scatter_third(step, gc, third16, gram_a, gram_b):
-        gc = gc - split_dot(third16, gram_a * gram_b)
+    def scatter_third(step, gc, third16, gram_ab):
+        gc = gc - split_dot(third16, gram_ab)
         c1s[step] = gc.reshape(Q, 4, rank)
         send(plane, lambda p: c1s.at[step, p], c1r.at[step], *plane_sems(step, PLANE_RS))
         c1r[step, q] = c1s[step, q]
@@ -233,7 +238,8 @@
         return own_a, own_b
 
     own_a, own_b = a_ref[...], b_ref[...]
-    third16, gram_c, norm_c = take_third(c_ref[...])
+    third16 = c_ref[...].astype(bf16)
+    gram_c, norm_c = take_third(third16)
     cq[...] = c_ref[...].reshape(Q, 4, rank)
     own_c = cq[q]
     pl.semaphore_wait(barrier, N - 1 + Q - 1)
@@ -249,8 +255,9 @@
     take_factors(0)
     gram_a, gram_b = grams(0)
     do_first_modes(0, gram_a, gram_b, gram_c)
+    send_norms(0)
     gc = third_mode(tt, ta32, tb16)
-    scatter_third(0, gc, third16, gram_a, gram_b)
+    scatter_third(0, gc, third16, split(gram_a * gram_b))
     step_a, step_b, step_c = sizes(0, norm_c)
     own_a, own_b = update_first(0, own_a, own_b, step_a, step_b)
     gather_factors(1, own_a, own_b)
@@ -259,9 +266,12 @@
     take_factors(1)
     gram_a, gram_b = grams(1)
     own_c = gather_third(0, own_c, step_c)
+    gram_ab = split(gram_a * gram_b)
     gc = third_mode(tt, ta32, tb16)
-    third16, gram_c, norm_c = take_third(whole_third(0))
-    scatter_third(1, gc, third16, gram_a, gram_b)
+    third16 = whole_third(0).astype(bf16)
+    scatter_third(1, gc, third16, gram_ab)
+    send_norms(1)
+    gram_c, norm_c = take_third(third16)
     do_first_modes(1, gram_a, gram_b, gram_c)
     line_third(1)
     step_a, step_b, step_c = sizes(1, norm_c)

time: 57.6 us -> 55.4 us (0.962)
  Pallas kernels: 56.8 us -> 54.6 us
    pallas_call x1, Pallas kernels: 55.3 us -> 53.1 us  [local(): pl.pallas_call(kernel, out_shape=[jax.ShapeDtypeStruct(x.shape, f32) for...]
where the time goes in v3:
time: 55.4 us; the launch traced here: 55.3 us
  Pallas kernels  54.6 us (99%)
  between operations  0.64 us (1%)
    pallas_call x1, Pallas kernels, local(): pl.pallas_call(kernel, out_shape=[jax.ShapeDtypeStruct(x.shape, f32) for...  53.1 us
    pallas_call x1, Pallas kernels, local(): pl.pallas_call(hand_over, out_shape=[jax.ShapeDtypeStruct(x.shape, f32) f...  1.5 us

profile of v3, /device:TPU:1, one launch (start us, length us, event | category | flops | bytes accessed | tf_op | source)
XLA Modules:
  0.0 55.3 jit_solution(17097314424058603342)
XLA Ops:
  0.6 53.1 %shard_map.67 = (f32[16,128]{1,0:T(8,128)}, f32[8,128]{1,0:T(8,128)}, f32[128,128]{1,0:T(8,128)}) custom-call(bf16[256,128,128]{2,1,0:T(8,128)(2,1)} %t_ref.1, f32[16,128]{1,0:T(8,128)} %a_ref.1, f32[8,128]{1,0:T(8,128)} %b_ref.1, f32[128,128]{1,0:T(8,128)} %c_ref.1), custom_call_target="tpu_custom_call" | custom-call | tf_op jit(solution)/shard_map/pallas_call | solution.py:300
  53.8 1.5 %shard_map.68 = (f32[16,128]{1,0:T(8,128)}, f32[8,128]{1,0:T(8,128)}, f32[128,128]{1,0:T(8,128)}) custom-call(f32[16,128]{1,0:T(8,128)} %get-tuple-element.6.a_ref, f32[8,128]{1,0:T(8,128)} %get-tuple-element.7.b_ref, f32[128,128]{1,0:T(8,128)} %get-tuple-element.8.c_ref), custom_call_target="tpu_custom_call" | custom-call | tf_op jit(solution)/shard_map/pallas_call | solution.py:342

commit v4 on v3

--- a/solution.py
+++ b/solution.py
@@ -186,10 +186,10 @@
     def do_first_modes(step, gram_a, gram_b, gram_c):
         gb = first_modes(tv, ta32, tb32, c16, ga)
         gb = gb - split_dot(tb16[...], split(gram_a * gram_c))
+        sb[step] = gb.reshape(N, 8, rank).astype(bf16)
+        send(rows, lambda p: sb.at[step, p], rb.at[step], *sems(step, RS_B))
         grad_a = ga[...] - split_dot(ta[step].reshape(rows_i, rank), split(gram_b * gram_c))
-        sb[step] = gb.reshape(N, 8, rank).astype(bf16)
         sa[step] = grad_a.astype(bf16).reshape(N, 16, rank)
-        send(rows, lambda p: sb.at[step, p], rb.at[step], *sems(step, RS_B))
         send(cols, lambda p: sa.at[step, p], ra.at[step], *sems(step, RS_A))
         rb[step, row] = sb[step, row]
         ra[step, col] = sa[step, col]
@@ -254,8 +254,8 @@
 
     take_factors(0)
     gram_a, gram_b = grams(0)
+    send_norms(0)
     do_first_modes(0, gram_a, gram_b, gram_c)
-    send_norms(0)
     gc = third_mode(tt, ta32, tb16)
     scatter_third(0, gc, third16, split(gram_a * gram_b))
     step_a, step_b, step_c = sizes(0, norm_c)

time: 55.4 us -> 55.3 us (level)
  no operation moved by 1% of the time
where the time goes in v4:
time: 55.3 us; the launch traced here: 55.1 us
  Pallas kernels  54.5 us (99%)
  between operations  0.64 us (1%)
    pallas_call x1, Pallas kernels, local(): pl.pallas_call(kernel, out_shape=[jax.ShapeDtypeStruct(x.shape, f32) for...  53 us
    pallas_call x1, Pallas kernels, local(): pl.pallas_call(hand_over, out_shape=[jax.ShapeDtypeStruct(x.shape, f32) f...  1.5 us

profile of v4, /device:TPU:1, one launch (start us, length us, event | category | flops | bytes accessed | tf_op | source)
XLA Modules:
  0.0 55.1 jit_solution(9490376416337317470)
XLA Ops:
  0.6 53.0 %shard_map.67 = (f32[16,128]{1,0:T(8,128)}, f32[8,128]{1,0:T(8,128)}, f32[128,128]{1,0:T(8,128)}) custom-call(bf16[256,128,128]{2,1,0:T(8,128)(2,1)} %t_ref.1, f32[16,128]{1,0:T(8,128)} %a_ref.1, f32[8,128]{1,0:T(8,128)} %b_ref.1, f32[128,128]{1,0:T(8,128)} %c_ref.1), custom_call_target="tpu_custom_call" | custom-call | tf_op jit(solution)/shard_map/pallas_call | solution.py:300
  53.6 1.5 %shard_map.68 = (f32[16,128]{1,0:T(8,128)}, f32[8,128]{1,0:T(8,128)}, f32[128,128]{1,0:T(8,128)}) custom-call(f32[16,128]{1,0:T(8,128)} %get-tuple-element.6.a_ref, f32[8,128]{1,0:T(8,128)} %get-tuple-element.7.b_ref, f32[128,128]{1,0:T(8,128)} %get-tuple-element.8.c_ref), custom_call_target="tpu_custom_call" | custom-call | tf_op jit(solution)/shard_map/pallas_call | solution.py:342
